TPU v7x, 32 devices: a whole 2x2x4 slice. The times are simulated.
32 devices in a mesh: grp: 2 (over y), user: 4 (over z), tm: 4 (over x, core).
Axes of the slice: x: 2, y: 2, z: 4, core: 2. Of those that a mesh axis runs over, the one named last changes fastest.
Arguments:
- history: bfloat16 [8, 1024, 512], P(('grp', 'user'), 'tm'), parts along dimension 0, may hold values from -6 to 6
- z_weight: bfloat16 [512, 1024], replicated, may hold values from -0.25 to 0.25
- xbc_weight: bfloat16 [512, 1280], replicated, may hold values from -0.25 to 0.25
- dt_weight: bfloat16 [512, 16], replicated, may hold values from -0.125 to 0.125
- dt_bias: float32 [16], replicated, may hold values from -1 to 0.5
- a_log: float32 [16], replicated
- conv_weight: float32 [4, 1280], replicated, may hold values from -3 to 3
- conv_bias: float32 [1280], replicated, may hold values from -3 to 3
- d_skip: float32 [16], replicated, may hold values from 0.5 to 1.5
- norm_gain: float32 [1024], replicated, may hold values from 0.1 to 1.9
- out_weight: bfloat16 [1024, 512], replicated, may hold values from -0.1875 to 0.1875
- label_pos: int32 [8, 2048], P(('grp', 'user'), 'tm'), parts along dimension 0, may hold values from 0 to 1023, as said below
- label_count: int32 [8, 4], P(('grp', 'user'), 'tm'), parts along dimension 0, may hold values from 1 to 511, as said below
- label_value: int32 [8, 2048], P(('grp', 'user'), 'tm'), parts along dimension 0, may hold values 0 or 1
- item_feat: bfloat16 [8, 2048, 512], P(('grp', 'user'), 'tm'), parts along dimension 0, may hold values from -6 to 6
- first_weight: bfloat16 [1024, 1024], replicated, may hold values from -0.1875 to 0.1875
- second_weight: bfloat16 [1024], replicated, may hold values from -0.1875 to 0.1875
Outputs:
- encoded: bfloat16 [8, 1024, 512], P(('grp', 'user'), 'tm'), parts along dimension 0
- row_logit: float32 [8, 2048], P(('grp', 'user'), 'tm'), parts along dimension 0
- grad_first: float32 [2048, 1024], P('grp'), parts along dimension 0
- grad_second: float32 [2048], P('grp'), parts along dimension 0
There are 2 independent parts, one for each index of `grp`. A program takes and returns all parts, laid end to end along the dimension named above; an argument that names none is the same for every part. Nothing has to cross between parts.
Inputs may be any that keep to these rules, and one draw needn't show every extreme that they name: `label_pos`: positions in slots k * 512 to (k + 1) * 512 - 1 of a user lie in events k * 256 to (k + 1) * 256 - 1. label_count[u, k] slots are used in block k of user u's slots, and they are the block's first ones; the counts of blocks 2 * k and 2 * k + 1 of a user sum to 512.
All inputs are finite; a program needn't handle non-finite values. No bound on the sum of `label_value` on one device may be relied on, other than what follows from the above.
Results may differ from a plain program's by a relative error of at most 0.015.
Values may be sent and summed in bfloat16 or wider, within the bound.
No kernel may reach another device: no remote copies, remote signals or barrier semaphores. Data moves between devices by JAX's collectives and lax.ppermute only.
A program may use at most 64 MiB of HBM per device.

v0:
```python
import jax
import jax.numpy as jnp
from jax import lax
from jax.sharding import PartitionSpec as P

BLOCK = 256


def passed_along(shard, axis, by):
    peers = lax.axis_size(axis)
    pairs = [(i, i + by) for i in range(peers) if 0 <= i + by < peers]
    return lax.ppermute(shard, axis, pairs)


def silu_grad(values):
    sig = jax.nn.sigmoid(values)
    return sig * (1.0 + values * (1.0 - sig))


def ranker(rank_rows, target, live_mask, first_weight, second_weight):
    pre_act = jnp.dot(rank_rows, first_weight, preferred_element_type=jnp.float32)
    hidden = jax.nn.silu(pre_act).astype(jnp.bfloat16)
    logit_vec = jnp.dot(hidden, second_weight, preferred_element_type=jnp.float32)
    dlogit = live_mask * (jax.nn.sigmoid(logit_vec) - target)
    grad_two = jnp.dot(dlogit, hidden.astype(jnp.float32), precision=lax.Precision.HIGHEST)
    grad_pre = (
        dlogit[:, None] * second_weight.astype(jnp.float32)[None, :] * silu_grad(pre_act)
    ).astype(jnp.bfloat16)
    grad_one = jnp.dot(rank_rows.T, grad_pre, preferred_element_type=jnp.float32)
    return (live_mask * logit_vec, grad_one, grad_two)


def body(
    history,
    z_weight,
    xbc_weight,
    dt_weight,
    dt_bias,
    a_log,
    conv_weight,
    conv_bias,
    d_skip,
    norm_gain,
    out_weight,
    label_pos,
    label_count,
    label_value,
    item_feat,
    first_weight,
    second_weight,
):
    user_count, length, model_width = history.shape
    inner_width = z_weight.shape[1]
    head_count = a_log.shape[0]
    head_size = inner_width // head_count
    state_dim = (xbc_weight.shape[1] - inner_width) // 2
    tap_count = conv_weight.shape[0]
    flat_rows = history.reshape(user_count * length, model_width)
    z_gate = (
        jnp.dot(flat_rows, z_weight, preferred_element_type=jnp.float32)
        .astype(jnp.bfloat16)
        .reshape(user_count, length, inner_width)
    )
    xbc_raw = (
        jnp.dot(flat_rows, xbc_weight, preferred_element_type=jnp.float32)
        .astype(jnp.bfloat16)
        .reshape(user_count, length, -1)
    )
    step_size = jax.nn.softplus(
        jnp.dot(flat_rows, dt_weight, preferred_element_type=jnp.float32) + dt_bias
    ).reshape(user_count, length, head_count)
    rim_rows = passed_along(xbc_raw[:, length - (tap_count - 1) :, :], "tm", 1)
    padded = jnp.concatenate([rim_rows, xbc_raw], axis=1)
    conv_sum = jnp.zeros(xbc_raw.shape, jnp.float32) + conv_bias
    for tap in range(tap_count):
        conv_sum = conv_sum + conv_weight[tap] * padded[:, tap : tap + length, :].astype(
            jnp.float32
        )
    xbc = jax.nn.silu(conv_sum).astype(jnp.bfloat16)
    block_count = length // BLOCK
    x_part = xbc[..., :inner_width].reshape(user_count, block_count, BLOCK, head_count, head_size)
    b_part = xbc[..., inner_width : inner_width + state_dim].reshape(
        user_count, block_count, BLOCK, state_dim
    )
    c_part = xbc[..., inner_width + state_dim :].reshape(user_count, block_count, BLOCK, state_dim)
    log_decay = (-jnp.exp(a_log) * step_size).reshape(user_count, block_count, BLOCK, head_count)
    cumulated = jnp.cumsum(log_decay, axis=2)
    step_blocks = step_size.reshape(user_count, block_count, BLOCK, head_count)
    rows_idx = lax.broadcasted_iota(jnp.int32, (BLOCK, BLOCK), 0)
    cols_idx = lax.broadcasted_iota(jnp.int32, (BLOCK, BLOCK), 1)
    causal = (cols_idx <= rows_idx)[None, None]

    def block_step(carry_state, inputs):
        x_block, b_block, c_block, cum_block, step_block = inputs
        scores = jnp.einsum("utn,usn->uts", c_block, b_block, preferred_element_type=jnp.float32)
        cum_heads = jnp.swapaxes(cum_block, 1, 2)
        gaps = cum_heads[:, :, :, None] - cum_heads[:, :, None, :]
        decays = jnp.where(causal, jnp.exp(jnp.where(causal, gaps, 0.0)), 0.0)
        weights = (decays * jnp.swapaxes(step_block, 1, 2)[:, :, None, :] * scores[:, None]).astype(
            jnp.bfloat16
        )
        within = jnp.einsum("uhts,ushp->uthp", weights, x_block, preferred_element_type=jnp.float32)
        last_cum = cum_block[:, -1, :]
        carried = (
            (jnp.exp(last_cum[:, None, :] - cum_block) * step_block)[..., None]
            * x_block.astype(jnp.float32)
        ).astype(jnp.bfloat16)
        new_state = jnp.exp(last_cum)[:, :, None, None] * carry_state + jnp.einsum(
            "ushp,usn->uhpn", carried, b_block, preferred_element_type=jnp.float32
        )
        result = within + d_skip[None, None, :, None] * x_block.astype(jnp.float32)
        return (new_state, (result, carry_state))

    zero_state = jnp.zeros((user_count, head_count, head_size, state_dim), jnp.float32)
    scan_inputs = (
        jnp.moveaxis(x_part, 1, 0),
        jnp.moveaxis(b_part, 1, 0),
        jnp.moveaxis(c_part, 1, 0),
        jnp.moveaxis(cumulated, 1, 0),
        jnp.moveaxis(step_blocks, 1, 0),
    )
    local_end, (partial_value, entering_local) = lax.scan(block_step, zero_state, scan_inputs)
    block_last = cumulated[:, :, -1, :]
    before_log = jnp.cumsum(block_last, axis=1) - block_last
    chain_gain = jnp.exp(jnp.sum(block_last, axis=1))
    incoming = jnp.zeros_like(local_end)
    for relay_step in range(lax.axis_size("tm") - 1):
        outgoing = chain_gain[:, :, None, None] * incoming + local_end
        incoming = passed_along(outgoing, "tm", 1)
    entering = (
        jnp.moveaxis(entering_local, 0, 1)
        + jnp.exp(before_log)[..., None, None] * incoming[:, None]
    )
    entering_high = entering.astype(jnp.bfloat16)
    entering_low = (entering - entering_high.astype(jnp.float32)).astype(jnp.bfloat16)
    state_read = jnp.einsum(
        "ubtn,ubhpn->ubthp", c_part, entering_high, preferred_element_type=jnp.float32
    )
    state_read = state_read + jnp.einsum(
        "ubtn,ubhpn->ubthp", c_part, entering_low, preferred_element_type=jnp.float32
    )
    across = jnp.exp(cumulated)[..., None] * state_read
    ssd_out = (jnp.moveaxis(partial_value, 0, 1) + across).reshape(user_count, length, inner_width)
    gated_out = ssd_out * jax.nn.silu(z_gate.astype(jnp.float32))
    normed = (
        gated_out
        * lax.rsqrt(jnp.mean(gated_out * gated_out, axis=-1, keepdims=True) + 1e-05)
        * norm_gain
    ).astype(jnp.bfloat16)
    encoded = (
        jnp.dot(normed.reshape(-1, inner_width), out_weight, preferred_element_type=jnp.float32)
        .astype(jnp.bfloat16)
        .reshape(user_count, length, model_width)
    )
    slot_count = label_pos.shape[1]
    tm_index = lax.axis_index("tm")
    local_pos = label_pos - tm_index * length
    enc_rows = jax.vmap(lambda table, indices: table[indices])(encoded, local_pos)
    rank_rows = jnp.concatenate([enc_rows, item_feat], axis=-1)
    slot_iota = lax.broadcasted_iota(jnp.int32, (user_count, slot_count), 1)
    live_mask = (slot_iota < label_count).astype(jnp.float32)
    target = label_value.astype(jnp.float32)
    logit_vec, grad_one, grad_two = ranker(
        rank_rows.reshape(-1, 2 * model_width),
        target.reshape(-1),
        live_mask.reshape(-1),
        first_weight,
        second_weight,
    )
    row_logit = logit_vec.reshape(user_count, slot_count)
    share_first, share_second = (
        lax.psum_scatter(
            grad_one.astype(jnp.bfloat16), "tm", scatter_dimension=0, tiled=True
        ).astype(jnp.float32),
        lax.psum_scatter(
            grad_two.astype(jnp.bfloat16), "tm", scatter_dimension=0, tiled=True
        ).astype(jnp.float32),
    )
    summed_first, summed_second = (
        lax.psum(share_first.astype(jnp.bfloat16), "user").astype(jnp.float32),
        lax.psum(share_second.astype(jnp.bfloat16), "user").astype(jnp.float32),
    )
    grad_first, grad_second = (
        lax.all_gather(summed_first.astype(jnp.bfloat16), "tm", axis=0, tiled=True).astype(
            summed_first.dtype
        ),
        lax.all_gather(summed_second.astype(jnp.bfloat16), "tm", axis=0, tiled=True).astype(
            summed_second.dtype
        ),
    )
    return (encoded, row_logit, grad_first, grad_second)


def solution(mesh):
    in_specs = (
        P(("grp", "user"), "tm", None),
        P(),
        P(),
        P(),
        P(),
        P(),
        P(),
        P(),
        P(),
        P(),
        P(),
        P(("grp", "user"), "tm"),
        P(("grp", "user"), "tm"),
        P(("grp", "user"), "tm"),
        P(("grp", "user"), "tm", None),
        P(),
        P(),
    )
    out_specs = (P(("grp", "user"), "tm", None), P(("grp", "user"), "tm"), P("grp", None), P("grp"))
    return jax.shard_map(body, mesh=mesh, in_specs=in_specs, out_specs=out_specs, check_vma=False)
```

profile of v0, /device:TPU:0, one launch (start us, length us, event | category | flops | bytes accessed | tf_op | source)
XLA Modules:
  0.0 186.1 jit_solution(1924651855535223238)
XLA Ops:
  7.3 2.0 %convolution_convert_fusion = bf16[256,1280]{1,0:T(8,128)(2,1)S(1)} fusion(bf16[512,1280]{1,0:T(8,128)(2,1)} %param.19, bf16[1,256,512]{2,1,0:T(8,128)(2,1)} %param.17), kind=kOutput, calls=%fused_computation.2 | convolution fusion | flops 335872000 | bytes 2228224 | tf_op jit(solution)/shard_map/dot_general | solution.py:65
  9.4 2.4 %collective-permute-start = (bf16[1,3,1280]{2,1,0:T(4,128)(2,1)S(1)}, bf16[1,3,1280]{2,1,0:T(4,128)(2,1)S(1)}, u32[]{:S(2)}, u32[]{:S(2)}) collective-permute-start(bf16[1,3,1280]{2,1,0:T(4,128)(2,1)S(1)} %slice.63), channel_id=1, source_target_pairs={{0,1},{1,2},{2,3},{4,5},{5,6},{6,7},{8,9},{9,10},{10,11},{12,13},{... | collective-permute-start | bytes 23048 | tf_op jit(solution)/shard_map/ppermute | solution.py:12
  11.8 0.2 compare_select_fusion
  12.1 0.6 reduce-window.6
  12.7 0.2 slice_reduce_fusion
  12.9 0.1 copy.40
  13.1 0.2 slice_reduce_fusion.1
  13.3 0.1 fusion.47
  13.4 0.2 exponential_reduce_fusion.1
  13.6 1.1 mul.297
  14.7 2.5 %copy.42 = f32[1,256,1024]{2,1,0:T(8,128)} copy(f32[1,256,1024]{1,2,0:T(8,128)} %bitcast.132) | data formatting | bytes 2097152 | tf_op jit(solution)/shard_map/while/body/eval_jaxpr/mul | solution.py:105
  17.3 0.9 multiply_convert_fusion.10
  18.2 0.3 copy-done.2
  18.5 0.1 multiply_convert_fusion.13
  18.6 1.0 copy.43
  19.6 1.4 convolution_add_fusion.1
  21.0 0.9 add_bitcast_fusion
  21.9 5.3 %collective-permute-start.1 = (f32[1,16,64,128]{3,2,1,0:T(8,128)}, f32[1,16,64,128]{3,2,1,0:T(8,128)}, u32[]{:S(2)}, u32[]{:S(2)}) collective-permute-start(f32[1,16,64,128]{3,2,1,0:T(8,128)} %add_bitcast_fusion), channel_id=1, source_target_pairs={{0,1},{1,2},{2,3},{4,5},{5,6},{6,7},{8,9},{9,10},{10,11},{12,13},{... | collective-permute-start | bytes 1572872 | tf_op jit(solution)/shard_map/ppermute | solution.py:12
  27.2 1.0 collective-permute-done.1
  28.3 2.0 %bitcast_add_fusion.2 = f32[1,16,64,128]{3,2,1,0:T(8,128)} fusion(f32[16,64,128]{2,1,0:T(8,128)S(1)} %convolution_add_fusion.1, f32[1,16,64,128]{3,2,1,0:T(8,128)} %collective-permute-done.1, f32[16]{0:T(128)S(1)} %get-tuple-element.31), kind=kLoop, calls=%fused_computation.47 | loop fusion | flops 262144 | bytes 1572928 | tf_op jit(solution)/shard_map/add | solution.py:128
  30.3 7.3 %collective-permute-start.2 = (f32[1,16,64,128]{3,2,1,0:T(8,128)}, f32[1,16,64,128]{3,2,1,0:T(8,128)}, u32[]{:S(2)}, u32[]{:S(2)}) collective-permute-start(f32[1,16,64,128]{3,2,1,0:T(8,128)} %bitcast_add_fusion.2), channel_id=1, source_target_pairs={{0,1},{1,2},{2,3},{4,5},{5,6},{6,7},{8,9},{9,10},{10,11},{12,13},{... | collective-permute-start | bytes 1572872 | tf_op jit(solution)/shard_map/ppermute | solution.py:12
  38.3 1.3 slice_convert_fusion
  39.6 2.6 %copy.41 = f32[1,256,1024]{1,2,0:T(8,128)} copy(f32[1,256,1024]{2,1,0:T(8,128)} %get-tuple-element.45) | data formatting | bytes 2097152 | tf_op jit(solution)/shard_map/while/body/eval_jaxpr/convert_element_type | solution.py:106
  42.1 2.0 %copy.37 = bf16[1,256,1024]{1,2,0:T(8,128)(2,1)} copy(bf16[1,256,1024]{2,1,0:T(8,128)(2,1)} %get-tuple-element.46) | data formatting | bytes 1048576 | tf_op jit(solution)/shard_map/slice | solution.py:81
  44.2 1.2 bitcast_add_fusion.1
  45.4 3.6 %collective-permute-start.3 = (f32[1,16,64,128]{3,2,1,0:T(8,128)S(1)}, f32[1,16,64,128]{3,2,1,0:T(8,128)S(1)}, u32[]{:S(2)}, u32[]{:S(2)}) collective-permute-start(f32[1,16,64,128]{3,2,1,0:T(8,128)S(1)} %bitcast_add_fusion.1), channel_id=1, source_target_pairs={{0,1},{1,2},{2,3},{4,5},{5,6},{6,7},{8,9},{9,10},{10,11},{12,13},{... | collective-permute-start | bytes 1572872 | tf_op jit(solution)/shard_map/ppermute | solution.py:12
  49.0 0.2 fusion.38
  49.2 2.8 %fusion.11 = f32[256,16,64]{0,2,1:T(8,128)S(1)} fusion(bf16[256,16,64]{0,2,1:T(8,128)(2,1)} %bitcast.138, f32[256,256]{1,0:T(8,128)S(1)} %fusion.38, f32[16,256]{1,0:T(8,128)S(1)} %bitcast.139, f32[16,256]{1,0:T(8,128)S(1)} %bitcast.142, pred[256,256]{1,0:T(8,128)(4,1)S(1)} %iota_compare_fusion, f32[1,256,16,64]{1,3,2,0:T(8,128)} %bitcast.135, ...), kind=kOutput, calls=%fused_computation.19 | convolution fusion | flops 141033472 | bytes 2981952 | tf_op jit(solution)/shard_map/while/body/eval_jaxpr/uhts,ushp->uthp/dot_general | solution.py:102
  52.0 0.3 fusion.28
  52.4 1.4 fusion.9
  53.8 2.5 %copy.44 = f32[256,1024]{1,0:T(8,128)} copy(f32[256,1024]{0,1:T(8,128)} %bitcast.133) | data formatting | bytes 2097152 | tf_op jit(solution)/shard_map/reshape | solution.py:143
  56.4 2.3 %multiply_reduce_fusion = (f32[256]{0:T(256)S(1)}, f32[256,1024]{1,0:T(8,128)S(1)}) fusion(f32[256,1024]{1,0:T(8,128)} %copy.44, bf16[512,1024]{1,0:T(8,128)(2,1)} %param.18, bf16[1,256,512]{2,1,0:T(8,128)(2,1)S(1)} %copy-done.4), kind=kOutput, calls=%fused_computation.38 | convolution fusion | flops 270794496 | bytes 3408896 | tf_op jit(solution)/shard_map/dot_general | solution.py:60
  58.7 0.5 fusion.12
  59.2 5.8 %gather_fusion = bf16[512,512]{1,0:T(8,128)(2,1)} fusion(bf16[1,256,512]{2,1,0:T(8,128)(2,1)S(1)} %fusion.12, s32[512]{0:T(512)S(1)} %bitcast.129), kind=kCustom, calls=%fused_computation | custom fusion | bytes 1052672 | tf_op jit(solution)/shard_map/vmap()/gather | solution.py:158
  65.0 2.8 %multiply_convert_fusion.3 = (bf16[512,1024]{1,0:T(8,128)(2,1)S(1)}, f32[512,1024]{1,0:T(8,128)S(1)}) fusion(bf16[1024,1024]{1,0:T(8,128)(2,1)S(1)} %copy-done, bf16[1,512,512]{2,1,0:T(8,128)(2,1)} %param.31, bf16[1,512,512]{2,1,0:T(8,128)(2,1)} %bitcast.136), kind=kOutput, calls=%fused_computation.5 | convolution fusion | flops 1078460416 | bytes 6291456 | tf_op jit(solution)/shard_map/dot_general | solution.py:21
  67.8 0.4 fusion.60
  68.2 0.6 fusion.54
  68.8 3.0 %convolution_convert_fusion.1 = bf16[1024,1024]{1,0:T(8,128)(2,1)} fusion(f32[512,1024]{1,0:T(8,128)S(1)} %get-tuple-element.52, f32[1024]{0:T(1024)S(1)} %convert_element_type.159, f32[512]{0:T(512)S(1)} %get-tuple-element.47, bf16[1,512,512]{2,1,0:T(8,128)(2,1)S(1)} %copy-done.15, bf16[1,512,512]{2,1,0:T(8,128)(2,1)S(1)} %bitcast.137), kind=kOutput, calls=%fused_computation.13 | convolution fusion | flops 1082130432 | bytes 5249024 | tf_op jit(solution)/shard_map/dot_general | solution.py:29
  71.9 38.7 %reduce-scatter.2.cloned.1.call-done = bf16[256,1024]{1,0:T(8,128)(2,1)} async-done(((bf16[1024,1024]{1,0:T(8,128)(2,1)}), bf16[256,1024]{1,0:T(8,128)(2,1)}) %reduce-scatter.2.cloned.1.call-update) | async-done | bytes 524304 | tf_op jit(solution)/shard_map/reduce_scatter | solution.py:172
  110.7 40.8 %all-reduce.3.cloned.1.call-done = bf16[256,1024]{1,0:T(8,128)(2,1)} async-done(((bf16[256,1024]{1,0:T(8,128)(2,1)}), bf16[256,1024]{1,0:T(8,128)(2,1)}) %all-reduce.3.cloned.1.call-update) | async-done | bytes 524304 | tf_op jit(solution)/shard_map/psum | solution.py:180
  151.5 0.6 dynamic-slice.3
  152.8 0.5 fusion.61
  153.3 5.6 %all-reduce = bf16[1024]{0:T(1024)(128)(2,1)S(1)} all-reduce(bf16[1024]{0:T(1024)(128)(2,1)S(1)} %convert_element_type.163), channel_id=3, replica_groups=mesh['grp'=2,'user'=4,'tm'=4] {'tm'}, use_global_device_ids=true, to_apply=%region_5.6.clone | all-reduce | flops 1024 | bytes 4096
  159.0 10.6 %psum.15 = bf16[256]{0:T(256)(128)(2,1)S(1)} all-reduce(bf16[256]{0:T(256)(128)(2,1)S(1)} %dynamic-slice.4), channel_id=1, replica_groups=mesh['grp'=2,'user'=4,'tm'=4] {'user'}, use_global_device_ids=true, to_apply=%region_6.7 | all-reduce | flops 256 | bytes 1024 | tf_op jit(solution)/shard_map/psum | solution.py:181
  169.6 5.1 %all-gather = bf16[4,1,256]{2,1,0:T(2,128)(2,1)S(1)} all-gather(bf16[1,1,256]{2,1,0:T(2,128)(2,1)S(1)} %reshape.326), channel_id=1, replica_groups=mesh['grp'=2,'user'=4,'tm'=4] {'tm'}, dimensions={0}, use_global_device_ids=true | all-gather | bytes 2560 | tf_op jit(solution)/shard_map/all_gather | solution.py:187
  174.7 0.6 convert_element_type.166
  175.3 0.2 all-gather.3.cloned.1.call-done
  175.5 4.1 %convert_element_type.162 = f32[1024,1024]{1,0:T(8,128)} convert(bf16[1024,1024]{1,0:T(8,128)(2,1)} %all-gather.3.cloned.1.call-done) | non-fusion elementwise | flops 1048576 | bytes 6291456 | tf_op jit(solution)/shard_map/convert_element_type | solution.py:184
  (68 shorter events, 0.7 us)
Async XLA Ops:
  7.2 57.8 %copy-start = (bf16[1024,1024]{1,0:T(8,128)(2,1)S(1)}, bf16[1024,1024]{1,0:T(8,128)(2,1)}, u32[]{:S(2)}) copy-start(bf16[1024,1024]{1,0:T(8,128)(2,1)} %param.32) | copy-start | bytes 6291460
  7.2 4.6 %copy-start.3 = (bf16[1,256,512]{2,1,0:T(8,128)(2,1)S(1)}, bf16[1,256,512]{2,1,0:T(8,128)(2,1)}, u32[]{:S(2)}) copy-start(bf16[1,256,512]{2,1,0:T(8,128)(2,1)} %param.17) | copy-start | bytes 786436
  7.2 4.6 %copy-start.16 = (f32[16]{0:T(128)S(1)}, f32[16]{0:T(128)}, u32[]{:S(2)}) copy-start(f32[16]{0:T(128)} %param.22) | copy-start | bytes 196
  7.2 4.6 %copy-start.14 = (f32[16]{0:T(128)S(1)}, f32[16]{0:T(128)}, u32[]{:S(2)}) copy-start(f32[16]{0:T(128)} %param.21) | copy-start | bytes 196
  7.2 4.6 %copy-start.8 = (bf16[512,16]{0,1:T(8,128)(2,1)S(1)}, bf16[512,16]{0,1:T(8,128)(2,1)}, u32[]{:S(2)}) copy-start(bf16[512,16]{0,1:T(8,128)(2,1)} %param.20) | copy-start | bytes 49156
  7.2 6.4 %copy-start.7 = (f32[4,1280]{1,0:T(4,128)S(1)}, f32[4,1280]{1,0:T(4,128)}, u32[]{:S(2)}) copy-start(f32[4,1280]{1,0:T(4,128)} %param.23) | copy-start | bytes 61444
  7.2 103.4 %reduce-scatter.2.cloned.1.call-start = ((), (), s32[]{:S(2)}) async-start(), calls=%async_computation.1 | async-start | bytes 2621440 | tf_op jit(solution)/shard_map/reduce_scatter | solution.py:172
  9.3 7.9 %copy-start.9 = (f32[1280]{0:T(1024)S(1)}, f32[1280]{0:T(1024)}, u32[]{:S(2)}) copy-start(f32[1280]{0:T(1024)} %param.24) | copy-start | bytes 15364
  9.4 7.9 %collective-permute-start = (bf16[1,3,1280]{2,1,0:T(4,128)(2,1)S(1)}, bf16[1,3,1280]{2,1,0:T(4,128)(2,1)S(1)}, u32[]{:S(2)}, u32[]{:S(2)}) collective-permute-start(bf16[1,3,1280]{2,1,0:T(4,128)(2,1)S(1)} %slice.63), channel_id=1, source_target_pairs={{0,1},{1,2},{2,3},{4,5},{5,6},{6,7},{8,9},{9,10},{10,11},{12,13},{... | collective-permute-start | bytes 23048 | tf_op jit(solution)/shard_map/ppermute | solution.py:12
  17.2 1.2 copy-start.2
  18.6 8.6 %copy-start.12 = (s32[1,512]{1,0:T(1,128)S(1)}, s32[1,512]{1,0:T(1,128)}, u32[]{:S(2)}) copy-start(s32[1,512]{1,0:T(1,128)} %param.28) | copy-start | bytes 6148
  19.6 17.9 %copy-start.10 = (bf16[1024]{0:T(1024)(128)(2,1)S(1)}, bf16[1024]{0:T(1024)(128)(2,1)}, u32[]{:S(2)}) copy-start(bf16[1024]{0:T(1024)(128)(2,1)} %param.33) | copy-start | bytes 6148
  19.6 18.6 %copy-start.13 = (s32[1,512]{1,0:T(1,128)S(1)}, s32[1,512]{1,0:T(1,128)}, u32[]{:S(2)}) copy-start(s32[1,512]{1,0:T(1,128)} %param.30) | copy-start | bytes 6148
  21.9 6.3 %collective-permute-start.1 = (f32[1,16,64,128]{3,2,1,0:T(8,128)}, f32[1,16,64,128]{3,2,1,0:T(8,128)}, u32[]{:S(2)}, u32[]{:S(2)}) collective-permute-start(f32[1,16,64,128]{3,2,1,0:T(8,128)} %add_bitcast_fusion), channel_id=1, source_target_pairs={{0,1},{1,2},{2,3},{4,5},{5,6},{6,7},{8,9},{9,10},{10,11},{12,13},{... | collective-permute-start | bytes 1572872 | tf_op jit(solution)/shard_map/ppermute | solution.py:12
  30.3 13.9 %collective-permute-start.2 = (f32[1,16,64,128]{3,2,1,0:T(8,128)}, f32[1,16,64,128]{3,2,1,0:T(8,128)}, u32[]{:S(2)}, u32[]{:S(2)}) collective-permute-start(f32[1,16,64,128]{3,2,1,0:T(8,128)} %bitcast_add_fusion.2), channel_id=1, source_target_pairs={{0,1},{1,2},{2,3},{4,5},{5,6},{6,7},{8,9},{9,10},{10,11},{12,13},{... | collective-permute-start | bytes 1572872 | tf_op jit(solution)/shard_map/ppermute | solution.py:12
  39.6 9.6 %copy-start.17 = (f32[16]{0:T(128)S(1)}, f32[16]{0:T(128)}, u32[]{:S(2)}) copy-start(f32[16]{0:T(128)} %param.25) | copy-start | bytes 196
  45.4 6.7 %collective-permute-start.3 = (f32[1,16,64,128]{3,2,1,0:T(8,128)S(1)}, f32[1,16,64,128]{3,2,1,0:T(8,128)S(1)}, u32[]{:S(2)}, u32[]{:S(2)}) collective-permute-start(f32[1,16,64,128]{3,2,1,0:T(8,128)S(1)} %bitcast_add_fusion.1), channel_id=1, source_target_pairs={{0,1},{1,2},{2,3},{4,5},{5,6},{6,7},{8,9},{9,10},{10,11},{12,13},{... | collective-permute-start | bytes 1572872 | tf_op jit(solution)/shard_map/ppermute | solution.py:12
  52.4 4.0 %copy-start.4 = (bf16[1,256,512]{2,1,0:T(8,128)(2,1)S(1)}, bf16[1,256,512]{2,1,0:T(8,128)(2,1)}, u32[]{:S(2)}) copy-start(bf16[1,256,512]{2,1,0:T(8,128)(2,1)} %param.17) | copy-start | bytes 786436
  56.4 2.3 %copy-start.5 = (bf16[1024,512]{1,0:T(8,128)(2,1)S(1)}, bf16[1024,512]{1,0:T(8,128)(2,1)}, u32[]{:S(2)}) copy-start(bf16[1024,512]{1,0:T(8,128)(2,1)} %param.27) | copy-start | bytes 3145732
  56.4 2.3 %copy-start.11 = (f32[1024]{0:T(1024)S(1)}, f32[1024]{0:T(1024)}, u32[]{:S(2)}) copy-start(f32[1024]{0:T(1024)} %param.26) | copy-start | bytes 12292
  59.2 5.8 %copy-start.1 = (bf16[1,256,512]{2,1,0:T(8,128)(2,1)}, bf16[1,256,512]{2,1,0:T(8,128)(2,1)S(1)}, u32[]{:S(2)}) copy-start(bf16[1,256,512]{2,1,0:T(8,128)(2,1)S(1)} %fusion.12) | copy-start | bytes 786436
  65.0 3.8 %copy-start.6 = (bf16[512,512]{1,0:T(8,128)(2,1)S(1)}, bf16[512,512]{1,0:T(8,128)(2,1)}, u32[]{:S(2)}) copy-start(bf16[512,512]{1,0:T(8,128)(2,1)} %gather_fusion) | copy-start | bytes 1572868
  65.0 3.8 %copy-start.15 = (bf16[1,512,512]{2,1,0:T(8,128)(2,1)S(1)}, bf16[1,512,512]{2,1,0:T(8,128)(2,1)}, u32[]{:S(2)}) copy-start(bf16[1,512,512]{2,1,0:T(8,128)(2,1)} %param.31) | copy-start | bytes 1572868
  71.8 79.7 %copy-start.18 = (u32[32]{0:T(128)S(1)}, u32[32]{0:T(128)}, u32[]{:S(2)}) copy-start(u32[32]{0:T(128)} %constant.78) | copy-start | bytes 388
  71.8 79.6 %all-reduce.3.cloned.1.call-start = ((), (), s32[]{:S(2)}) async-start(), calls=%async_computation.2 | async-start | bytes 1048576 | tf_op jit(solution)/shard_map/psum | solution.py:180
  110.6 64.9 %all-gather.3.cloned.1.call-start = ((), (), s32[]{:S(2)}) async-start(), calls=%async_computation.3 | async-start | bytes 2621440 | tf_op jit(solution)/shard_map/all_gather | solution.py:184
Sparse Core Ops, SparseCore 0:
  72.0 38.5 reduce-scatter.1
  112.9 38.4 all-reduce.2
  153.0 22.3 all-gather.2
where the time goes:
time: 187 us; the launch traced here: 186 us
  waiting for transfers between devices  80.8 us (43%)
  blocking collectives  21.3 us (11%)
  local copies, waits for them, and re-layouts  19.2 us (10%)
  starting transfers between devices  18.7 us (10%)
  matrix products  17.8 us (10%)
  between operations  15.4 us (8%)
  other arithmetic  12.8 us (7%)
    psum x1, waiting for transfers between devices, body(): lax.psum(share_first.astype(jnp.bfloat16), 'user').astype(jnp.float32)  40.8 us
    reduce_scatter x1, waiting for transfers between devices, body(): lax.psum_scatter(grad_one.astype(jnp.bfloat16), 'tm', scatter_dimension=0...  38.7 us
    ppermute x4, starting transfers between devices, passed_along(): return lax.ppermute(shard, axis, pairs)  18.6 us
    psum x1, blocking collectives, body(): lax.psum(share_second.astype(jnp.bfloat16), 'user').astype(jnp.float32)  10.6 us
    gather x2, local copies, waits for them, and re-layouts, body(): table[indices]  5.84 us
    unnamed x1, blocking collectives  5.65 us
    all_gather x1, blocking collectives, body(): lax.all_gather(summed_second.astype(jnp.bfloat16), 'tm', axis=0, tiled=True)  5.13 us
    convert_element_type x1, other arithmetic, body(): lax.all_gather(summed_first.astype(jnp.bfloat16), 'tm', axis=0, tiled=True)  4.07 us
  transfers between devices with their start and end apart: 7, of which 4 were waited for; matrix products, arithmetic and copies ran while one was open for 9% of the time, Pallas kernels for 0%

commit v1 on v0

--- a/solution.py
+++ b/solution.py
@@ -176,8 +176,9 @@
             grad_two.astype(jnp.bfloat16), "tm", scatter_dimension=0, tiled=True
         ).astype(jnp.float32),
     )
+    _number_slot = lambda piece_in, lane_axis: lax.all_gather(piece_in, lane_axis).sum(axis=0)
     summed_first, summed_second = (
-        lax.psum(share_first.astype(jnp.bfloat16), "user").astype(jnp.float32),
+        _number_slot(share_first.astype(jnp.bfloat16), "user").astype(jnp.float32),
         lax.psum(share_second.astype(jnp.bfloat16), "user").astype(jnp.float32),
     )
     grad_first, grad_second = (

time: 187 us -> 196 us (1.048)
  waiting for transfers between devices: 80.8 us -> 87 us
  other arithmetic: 12.8 us -> 15.7 us
    all_gather x0 -> x1, waiting for transfers between devices: none -> 47.2 us  [body(): lax.all_gather(piece_in, lane_axis).sum(axis=0)]
    psum x1 -> x0, waiting for transfers between devices: 40.8 us -> none  [body(): lax.psum(share_first.astype(jnp.bfloat16), 'user').astype(jnp.float32)]
    reduce_sum x0 -> x1, other arithmetic: none -> 2.92 us  [body(): lax.all_gather(piece_in, lane_axis).sum(axis=0)]
  transfers between devices with their start and end apart: 7 -> 7, of which waited for: 4 -> 3; matrix products, arithmetic and copies ran while one was open for 9% -> 8% of each run, Pallas kernels for 0% -> 0%
where the time goes in v1:
time: 196 us; the launch traced here: 195 us
  waiting for transfers between devices  87 us (44%)
  blocking collectives  21.4 us (11%)
  local copies, waits for them, and re-layouts  19.2 us (10%)
  starting transfers between devices  18.7 us (10%)
  matrix products  17.8 us (9%)
  other arithmetic  15.7 us (8%)
  between operations  15.5 us (8%)
    all_gather x1, waiting for transfers between devices, body(): lax.all_gather(piece_in, lane_axis).sum(axis=0)  47.2 us
    reduce_scatter x1, waiting for transfers between devices, body(): lax.psum_scatter(grad_one.astype(jnp.bfloat16), 'tm', scatter_dimension=0...  38.7 us
    ppermute x4, starting transfers between devices, passed_along(): return lax.ppermute(shard, axis, pairs)  18.6 us
    psum x1, blocking collectives, body(): lax.psum(share_second.astype(jnp.bfloat16), 'user').astype(jnp.float32)  9.94 us
    unnamed x1, blocking collectives  6.37 us
    gather x2, local copies, waits for them, and re-layouts, body(): table[indices]  5.84 us
    all_gather x1, blocking collectives, body(): lax.all_gather(summed_second.astype(jnp.bfloat16), 'tm', axis=0, tiled=True)  5.06 us
    convert_element_type x1, other arithmetic, body(): lax.all_gather(summed_first.astype(jnp.bfloat16), 'tm', axis=0, tiled=True)  4.07 us
  transfers between devices with their start and end apart: 7, of which 3 were waited for; matrix products, arithmetic and copies ran while one was open for 8% of the time, Pallas kernels for 0%

profile of v1, /device:TPU:0, one launch (start us, length us, event | category | flops | bytes accessed | tf_op | source)
XLA Modules:
  0.0 195.2 jit_solution(10576400393051169997)
XLA Ops:
  7.3 2.0 %convolution_convert_fusion = bf16[256,1280]{1,0:T(8,128)(2,1)S(1)} fusion(bf16[512,1280]{1,0:T(8,128)(2,1)} %param.19, bf16[1,256,512]{2,1,0:T(8,128)(2,1)} %param.17), kind=kOutput, calls=%fused_computation.2 | convolution fusion | flops 335872000 | bytes 2228224 | tf_op jit(solution)/shard_map/dot_general | solution.py:65
  9.4 2.4 %collective-permute-start = (bf16[1,3,1280]{2,1,0:T(4,128)(2,1)S(1)}, bf16[1,3,1280]{2,1,0:T(4,128)(2,1)S(1)}, u32[]{:S(2)}, u32[]{:S(2)}) collective-permute-start(bf16[1,3,1280]{2,1,0:T(4,128)(2,1)S(1)} %slice.63), channel_id=1, source_target_pairs={{0,1},{1,2},{2,3},{4,5},{5,6},{6,7},{8,9},{9,10},{10,11},{12,13},{... | collective-permute-start | bytes 23048 | tf_op jit(solution)/shard_map/ppermute | solution.py:12
  11.8 0.2 compare_select_fusion
  12.1 0.6 reduce-window.6
  12.7 0.2 slice_reduce_fusion
  12.9 0.1 copy.40
  13.1 0.2 slice_reduce_fusion.1
  13.3 0.1 fusion.47
  13.4 0.2 exponential_reduce_fusion.1
  13.6 1.1 mul.297
  14.7 2.5 %copy.42 = f32[1,256,1024]{2,1,0:T(8,128)} copy(f32[1,256,1024]{1,2,0:T(8,128)} %bitcast.133) | data formatting | bytes 2097152 | tf_op jit(solution)/shard_map/while/body/eval_jaxpr/mul | solution.py:105
  17.3 0.9 multiply_convert_fusion.10
  18.2 0.3 copy-done.2
  18.5 0.1 multiply_convert_fusion.13
  18.6 1.0 copy.43
  19.6 1.4 convolution_add_fusion.1
  21.0 0.9 add_bitcast_fusion
  21.9 5.3 %collective-permute-start.1 = (f32[1,16,64,128]{3,2,1,0:T(8,128)}, f32[1,16,64,128]{3,2,1,0:T(8,128)}, u32[]{:S(2)}, u32[]{:S(2)}) collective-permute-start(f32[1,16,64,128]{3,2,1,0:T(8,128)} %add_bitcast_fusion), channel_id=1, source_target_pairs={{0,1},{1,2},{2,3},{4,5},{5,6},{6,7},{8,9},{9,10},{10,11},{12,13},{... | collective-permute-start | bytes 1572872 | tf_op jit(solution)/shard_map/ppermute | solution.py:12
  27.2 1.0 collective-permute-done.1
  28.3 2.0 %bitcast_add_fusion.2 = f32[1,16,64,128]{3,2,1,0:T(8,128)} fusion(f32[16,64,128]{2,1,0:T(8,128)S(1)} %convolution_add_fusion.1, f32[1,16,64,128]{3,2,1,0:T(8,128)} %collective-permute-done.1, f32[16]{0:T(128)S(1)} %get-tuple-element.31), kind=kLoop, calls=%fused_computation.47 | loop fusion | flops 262144 | bytes 1572928 | tf_op jit(solution)/shard_map/add | solution.py:128
  30.3 7.3 %collective-permute-start.2 = (f32[1,16,64,128]{3,2,1,0:T(8,128)}, f32[1,16,64,128]{3,2,1,0:T(8,128)}, u32[]{:S(2)}, u32[]{:S(2)}) collective-permute-start(f32[1,16,64,128]{3,2,1,0:T(8,128)} %bitcast_add_fusion.2), channel_id=1, source_target_pairs={{0,1},{1,2},{2,3},{4,5},{5,6},{6,7},{8,9},{9,10},{10,11},{12,13},{... | collective-permute-start | bytes 1572872 | tf_op jit(solution)/shard_map/ppermute | solution.py:12
  38.3 1.3 slice_convert_fusion
  39.6 2.6 %copy.41 = f32[1,256,1024]{1,2,0:T(8,128)} copy(f32[1,256,1024]{2,1,0:T(8,128)} %get-tuple-element.45) | data formatting | bytes 2097152 | tf_op jit(solution)/shard_map/while/body/eval_jaxpr/convert_element_type | solution.py:106
  42.1 2.0 %copy.37 = bf16[1,256,1024]{1,2,0:T(8,128)(2,1)} copy(bf16[1,256,1024]{2,1,0:T(8,128)(2,1)} %get-tuple-element.46) | data formatting | bytes 1048576 | tf_op jit(solution)/shard_map/slice | solution.py:81
  44.2 1.2 bitcast_add_fusion.1
  45.4 3.6 %collective-permute-start.3 = (f32[1,16,64,128]{3,2,1,0:T(8,128)S(1)}, f32[1,16,64,128]{3,2,1,0:T(8,128)S(1)}, u32[]{:S(2)}, u32[]{:S(2)}) collective-permute-start(f32[1,16,64,128]{3,2,1,0:T(8,128)S(1)} %bitcast_add_fusion.1), channel_id=1, source_target_pairs={{0,1},{1,2},{2,3},{4,5},{5,6},{6,7},{8,9},{9,10},{10,11},{12,13},{... | collective-permute-start | bytes 1572872 | tf_op jit(solution)/shard_map/ppermute | solution.py:12
  49.0 0.2 fusion.38
  49.2 2.8 %fusion.11 = f32[256,16,64]{0,2,1:T(8,128)S(1)} fusion(bf16[256,16,64]{0,2,1:T(8,128)(2,1)} %bitcast.140, f32[256,256]{1,0:T(8,128)S(1)} %fusion.38, f32[16,256]{1,0:T(8,128)S(1)} %bitcast.141, f32[16,256]{1,0:T(8,128)S(1)} %bitcast.144, pred[256,256]{1,0:T(8,128)(4,1)S(1)} %iota_compare_fusion, f32[1,256,16,64]{1,3,2,0:T(8,128)} %bitcast.137, ...), kind=kOutput, calls=%fused_computation.19 | convolution fusion | flops 141033472 | bytes 2981952 | tf_op jit(solution)/shard_map/while/body/eval_jaxpr/uhts,ushp->uthp/dot_general | solution.py:102
  52.0 0.3 fusion.28
  52.4 1.4 fusion.9
  53.8 2.5 %copy.44 = f32[256,1024]{1,0:T(8,128)} copy(f32[256,1024]{0,1:T(8,128)} %bitcast.134) | data formatting | bytes 2097152 | tf_op jit(solution)/shard_map/reshape | solution.py:143
  56.4 2.3 %multiply_reduce_fusion = (f32[256]{0:T(256)S(1)}, f32[256,1024]{1,0:T(8,128)S(1)}) fusion(f32[256,1024]{1,0:T(8,128)} %copy.44, bf16[512,1024]{1,0:T(8,128)(2,1)} %param.18, bf16[1,256,512]{2,1,0:T(8,128)(2,1)S(1)} %copy-done.4), kind=kOutput, calls=%fused_computation.38 | convolution fusion | flops 270794496 | bytes 3408896 | tf_op jit(solution)/shard_map/dot_general | solution.py:60
  58.7 0.5 fusion.12
  59.2 5.8 %gather_fusion = bf16[512,512]{1,0:T(8,128)(2,1)} fusion(bf16[1,256,512]{2,1,0:T(8,128)(2,1)S(1)} %fusion.12, s32[512]{0:T(512)S(1)} %bitcast.130), kind=kCustom, calls=%fused_computation | custom fusion | bytes 1052672 | tf_op jit(solution)/shard_map/vmap()/gather | solution.py:158
  65.0 2.8 %multiply_convert_fusion.3 = (bf16[512,1024]{1,0:T(8,128)(2,1)S(1)}, f32[512,1024]{1,0:T(8,128)S(1)}) fusion(bf16[1024,1024]{1,0:T(8,128)(2,1)S(1)} %copy-done, bf16[1,512,512]{2,1,0:T(8,128)(2,1)} %param.31, bf16[1,512,512]{2,1,0:T(8,128)(2,1)} %bitcast.138), kind=kOutput, calls=%fused_computation.5 | convolution fusion | flops 1078460416 | bytes 6291456 | tf_op jit(solution)/shard_map/dot_general | solution.py:21
  67.8 0.4 fusion.60
  68.2 0.6 fusion.54
  68.8 3.0 %convolution_convert_fusion.1 = bf16[1024,1024]{1,0:T(8,128)(2,1)} fusion(f32[512,1024]{1,0:T(8,128)S(1)} %get-tuple-element.52, f32[1024]{0:T(1024)S(1)} %convert_element_type.161, f32[512]{0:T(512)S(1)} %get-tuple-element.47, bf16[1,512,512]{2,1,0:T(8,128)(2,1)S(1)} %copy-done.15, bf16[1,512,512]{2,1,0:T(8,128)(2,1)S(1)} %bitcast.139), kind=kOutput, calls=%fused_computation.13 | convolution fusion | flops 1082130432 | bytes 5249024 | tf_op jit(solution)/shard_map/dot_general | solution.py:29
  71.9 38.7 %reduce-scatter.2.cloned.1.call-done = bf16[256,1024]{1,0:T(8,128)(2,1)} async-done(((bf16[1024,1024]{1,0:T(8,128)(2,1)}), bf16[256,1024]{1,0:T(8,128)(2,1)}) %reduce-scatter.2.cloned.1.call-update) | async-done | bytes 524304 | tf_op jit(solution)/shard_map/reduce_scatter | solution.py:172
  110.7 47.2 %all-gather.7.cloned.1.call-done = bf16[1024,1024]{1,0:T(8,128)(2,1)} async-done(((bf16[256,1024]{1,0:T(8,128)(2,1)}), bf16[1024,1024]{1,0:T(8,128)(2,1)}) %all-gather.7.cloned.1.call-update) | async-done | bytes 2097168 | tf_op jit(solution)/shard_map/all_gather | solution.py:179
  157.8 2.9 %reduce_sum.26 = bf16[256,1024]{1,0:T(8,128)(2,1)} reduce(bf16[4,256,1024]{2,1,0:T(8,128)(2,1)} %bitcast.135, bf16[]{:T(256)} %constant.58.clone.1), dimensions={0}, to_apply=%region_4.5 | reduce | flops 786432 | bytes 2621442 | tf_op jit(solution)/shard_map/reduce_sum | solution.py:179
  160.8 0.6 dynamic-slice.3
  162.0 0.5 fusion.61
  162.6 6.4 %all-reduce = bf16[1024]{0:T(1024)(128)(2,1)S(1)} all-reduce(bf16[1024]{0:T(1024)(128)(2,1)S(1)} %convert_element_type.165), channel_id=4, replica_groups=mesh['grp'=2,'user'=4,'tm'=4] {'tm'}, use_global_device_ids=true, to_apply=%region_5.6.clone | all-reduce | flops 1024 | bytes 4096
  169.0 9.9 %psum.7 = bf16[256]{0:T(256)(128)(2,1)S(1)} all-reduce(bf16[256]{0:T(256)(128)(2,1)S(1)} %dynamic-slice.4), channel_id=1, replica_groups=mesh['grp'=2,'user'=4,'tm'=4] {'user'}, use_global_device_ids=true, to_apply=%region_6.7 | all-reduce | flops 256 | bytes 1024 | tf_op jit(solution)/shard_map/psum | solution.py:182
  179.0 5.1 %all-gather.1 = bf16[4,1,256]{2,1,0:T(2,128)(2,1)S(1)} all-gather(bf16[1,1,256]{2,1,0:T(2,128)(2,1)S(1)} %reshape.327), channel_id=1, replica_groups=mesh['grp'=2,'user'=4,'tm'=4] {'tm'}, dimensions={0}, use_global_device_ids=true | all-gather | bytes 2560 | tf_op jit(solution)/shard_map/all_gather | solution.py:188
  184.0 0.6 convert_element_type.168
  184.6 4.1 %convert_element_type.164 = f32[1024,1024]{1,0:T(8,128)} convert(bf16[1024,1024]{1,0:T(8,128)(2,1)} %all-gather.5.cloned.1.call-done) | non-fusion elementwise | flops 1048576 | bytes 6291456 | tf_op jit(solution)/shard_map/convert_element_type | solution.py:185
  (69 shorter events, 0.8 us)
Async XLA Ops:
  7.2 57.8 %copy-start = (bf16[1024,1024]{1,0:T(8,128)(2,1)S(1)}, bf16[1024,1024]{1,0:T(8,128)(2,1)}, u32[]{:S(2)}) copy-start(bf16[1024,1024]{1,0:T(8,128)(2,1)} %param.32) | copy-start | bytes 6291460
  7.2 4.6 %copy-start.3 = (bf16[1,256,512]{2,1,0:T(8,128)(2,1)S(1)}, bf16[1,256,512]{2,1,0:T(8,128)(2,1)}, u32[]{:S(2)}) copy-start(bf16[1,256,512]{2,1,0:T(8,128)(2,1)} %param.17) | copy-start | bytes 786436
  7.2 4.6 %copy-start.16 = (f32[16]{0:T(128)S(1)}, f32[16]{0:T(128)}, u32[]{:S(2)}) copy-start(f32[16]{0:T(128)} %param.22) | copy-start | bytes 196
  7.2 4.6 %copy-start.14 = (f32[16]{0:T(128)S(1)}, f32[16]{0:T(128)}, u32[]{:S(2)}) copy-start(f32[16]{0:T(128)} %param.21) | copy-start | bytes 196
  7.2 4.6 %copy-start.8 = (bf16[512,16]{0,1:T(8,128)(2,1)S(1)}, bf16[512,16]{0,1:T(8,128)(2,1)}, u32[]{:S(2)}) copy-start(bf16[512,16]{0,1:T(8,128)(2,1)} %param.20) | copy-start | bytes 49156
  7.2 6.4 %copy-start.7 = (f32[4,1280]{1,0:T(4,128)S(1)}, f32[4,1280]{1,0:T(4,128)}, u32[]{:S(2)}) copy-start(f32[4,1280]{1,0:T(4,128)} %param.23) | copy-start | bytes 61444
  7.2 103.3 %reduce-scatter.2.cloned.1.call-start = ((), (), s32[]{:S(2)}) async-start(), calls=%async_computation.1 | async-start | bytes 2621440 | tf_op jit(solution)/shard_map/reduce_scatter | solution.py:172
  9.3 7.9 %copy-start.9 = (f32[1280]{0:T(1024)S(1)}, f32[1280]{0:T(1024)}, u32[]{:S(2)}) copy-start(f32[1280]{0:T(1024)} %param.24) | copy-start | bytes 15364
  9.4 7.9 %collective-permute-start = (bf16[1,3,1280]{2,1,0:T(4,128)(2,1)S(1)}, bf16[1,3,1280]{2,1,0:T(4,128)(2,1)S(1)}, u32[]{:S(2)}, u32[]{:S(2)}) collective-permute-start(bf16[1,3,1280]{2,1,0:T(4,128)(2,1)S(1)} %slice.63), channel_id=1, source_target_pairs={{0,1},{1,2},{2,3},{4,5},{5,6},{6,7},{8,9},{9,10},{10,11},{12,13},{... | collective-permute-start | bytes 23048 | tf_op jit(solution)/shard_map/ppermute | solution.py:12
  17.2 1.2 copy-start.2
  18.6 8.6 %copy-start.12 = (s32[1,512]{1,0:T(1,128)S(1)}, s32[1,512]{1,0:T(1,128)}, u32[]{:S(2)}) copy-start(s32[1,512]{1,0:T(1,128)} %param.28) | copy-start | bytes 6148
  19.6 17.9 %copy-start.10 = (bf16[1024]{0:T(1024)(128)(2,1)S(1)}, bf16[1024]{0:T(1024)(128)(2,1)}, u32[]{:S(2)}) copy-start(bf16[1024]{0:T(1024)(128)(2,1)} %param.33) | copy-start | bytes 6148
  19.6 18.6 %copy-start.13 = (s32[1,512]{1,0:T(1,128)S(1)}, s32[1,512]{1,0:T(1,128)}, u32[]{:S(2)}) copy-start(s32[1,512]{1,0:T(1,128)} %param.30) | copy-start | bytes 6148
  21.9 6.3 %collective-permute-start.1 = (f32[1,16,64,128]{3,2,1,0:T(8,128)}, f32[1,16,64,128]{3,2,1,0:T(8,128)}, u32[]{:S(2)}, u32[]{:S(2)}) collective-permute-start(f32[1,16,64,128]{3,2,1,0:T(8,128)} %add_bitcast_fusion), channel_id=1, source_target_pairs={{0,1},{1,2},{2,3},{4,5},{5,6},{6,7},{8,9},{9,10},{10,11},{12,13},{... | collective-permute-start | bytes 1572872 | tf_op jit(solution)/shard_map/ppermute | solution.py:12
  30.3 13.9 %collective-permute-start.2 = (f32[1,16,64,128]{3,2,1,0:T(8,128)}, f32[1,16,64,128]{3,2,1,0:T(8,128)}, u32[]{:S(2)}, u32[]{:S(2)}) collective-permute-start(f32[1,16,64,128]{3,2,1,0:T(8,128)} %bitcast_add_fusion.2), channel_id=1, source_target_pairs={{0,1},{1,2},{2,3},{4,5},{5,6},{6,7},{8,9},{9,10},{10,11},{12,13},{... | collective-permute-start | bytes 1572872 | tf_op jit(solution)/shard_map/ppermute | solution.py:12
  39.6 9.6 %copy-start.17 = (f32[16]{0:T(128)S(1)}, f32[16]{0:T(128)}, u32[]{:S(2)}) copy-start(f32[16]{0:T(128)} %param.25) | copy-start | bytes 196
  45.4 6.7 %collective-permute-start.3 = (f32[1,16,64,128]{3,2,1,0:T(8,128)S(1)}, f32[1,16,64,128]{3,2,1,0:T(8,128)S(1)}, u32[]{:S(2)}, u32[]{:S(2)}) collective-permute-start(f32[1,16,64,128]{3,2,1,0:T(8,128)S(1)} %bitcast_add_fusion.1), channel_id=1, source_target_pairs={{0,1},{1,2},{2,3},{4,5},{5,6},{6,7},{8,9},{9,10},{10,11},{12,13},{... | collective-permute-start | bytes 1572872 | tf_op jit(solution)/shard_map/ppermute | solution.py:12
  52.4 4.0 %copy-start.4 = (bf16[1,256,512]{2,1,0:T(8,128)(2,1)S(1)}, bf16[1,256,512]{2,1,0:T(8,128)(2,1)}, u32[]{:S(2)}) copy-start(bf16[1,256,512]{2,1,0:T(8,128)(2,1)} %param.17) | copy-start | bytes 786436
  56.4 2.3 %copy-start.5 = (bf16[1024,512]{1,0:T(8,128)(2,1)S(1)}, bf16[1024,512]{1,0:T(8,128)(2,1)}, u32[]{:S(2)}) copy-start(bf16[1024,512]{1,0:T(8,128)(2,1)} %param.27) | copy-start | bytes 3145732
  56.4 2.3 %copy-start.11 = (f32[1024]{0:T(1024)S(1)}, f32[1024]{0:T(1024)}, u32[]{:S(2)}) copy-start(f32[1024]{0:T(1024)} %param.26) | copy-start | bytes 12292
  59.2 5.8 %copy-start.1 = (bf16[1,256,512]{2,1,0:T(8,128)(2,1)}, bf16[1,256,512]{2,1,0:T(8,128)(2,1)S(1)}, u32[]{:S(2)}) copy-start(bf16[1,256,512]{2,1,0:T(8,128)(2,1)S(1)} %fusion.12) | copy-start | bytes 786436
  65.0 3.8 %copy-start.6 = (bf16[512,512]{1,0:T(8,128)(2,1)S(1)}, bf16[512,512]{1,0:T(8,128)(2,1)}, u32[]{:S(2)}) copy-start(bf16[512,512]{1,0:T(8,128)(2,1)} %gather_fusion) | copy-start | bytes 1572868
  65.0 3.8 %copy-start.15 = (bf16[1,512,512]{2,1,0:T(8,128)(2,1)S(1)}, bf16[1,512,512]{2,1,0:T(8,128)(2,1)}, u32[]{:S(2)}) copy-start(bf16[1,512,512]{2,1,0:T(8,128)(2,1)} %param.31) | copy-start | bytes 1572868
  71.8 89.0 %copy-start.18 = (u32[32]{0:T(128)S(1)}, u32[32]{0:T(128)}, u32[]{:S(2)}) copy-start(u32[32]{0:T(128)} %constant.80) | copy-start | bytes 388
  71.8 86.0 %all-gather.7.cloned.1.call-start = ((), (), s32[]{:S(2)}) async-start(), calls=%async_computation.3 | async-start | bytes 2621440 | tf_op jit(solution)/shard_map/all_gather | solution.py:179
  110.6 74.0 %all-gather.5.cloned.1.call-start = ((), (), s32[]{:S(2)}) async-start(), calls=%async_computation.2 | async-start | bytes 2621440 | tf_op jit(solution)/shard_map/all_gather | solution.py:185
Sparse Core Ops, SparseCore 0:
  71.9 38.5 reduce-scatter.1
  112.2 45.6 all-gather.6
  160.9 21.3 all-gather.4
